TPU v7x, 32 devices: a whole 2x2x4 slice. The times are simulated.
32 devices in a mesh: row: 8 (over y, x, core), col: 4 (over z).
Axes of the slice: x: 2, y: 2, z: 4, core: 2. Of those that a mesh axis runs over, the one named last changes fastest.
Arguments:
- col_samples: float32 [16, 2, 2048, 128], P('row', None, 'col'), may hold values from -6 to 6
- row_samples: float32 [16, 2, 128, 2048], P('row', None, None, 'col'), may hold values from -6 to 6
- pivot_rows: int32 [16, 128], P('row'), may hold values from 0 to 2047
- rank_blocks: int32 [16], P('row'), may hold values from 1 to 8
- upper_inverse: float32 [2, 2048, 2048], P(None, 'col', 'row'), as said below
- upanel_left: float32 [4, 2, 2048, 128], P('col'), may hold values from -0.125 to 0.125
Outputs:
- panel_right: float32 [16, 2, 128, 2048], P('row', None, None, 'col')
- cores: float32 [16, 4, 2, 128, 128], P('row', 'col')
Inputs may be any that keep to these rules, and one draw needn't show every extreme that they name: `rank_blocks`: the tile's rank is 16 times this. `upper_inverse`: zero below the diagonal in both parts.
All inputs are finite; a program needn't handle non-finite values.
Results may differ from a plain program's by a relative error of at most 0.00007.
Values sent between devices are 32-bit elements; how exact they have to be, the bound alone decides.
A program may use at most 64 MiB of HBM per device.

v0:
```python
import jax
import jax.numpy as jnp
from jax import lax
from jax.sharding import PartitionSpec as P

RANK_STEP = 16


def complex_product(pattern, left_real, left_imag, right_real, right_imag):

    def single(left, right):
        return jnp.einsum(
            pattern,
            left,
            right,
            precision=lax.Precision.HIGHEST,
            preferred_element_type=jnp.float32,
        )

    real_part = single(left_real, right_real) - single(left_imag, right_imag)
    imag_part = single(left_real, right_imag) + single(left_imag, right_real)
    return (real_part, imag_part)


def scale_rows(values, weight_real, weight_imag):
    wr = weight_real[:, :, None]
    wi = weight_imag[:, :, None]
    real_part = values[:, 0] * wr - values[:, 1] * wi
    imag_part = values[:, 0] * wi + values[:, 1] * wr
    return jnp.stack((real_part, imag_part), axis=1)


def on_device(col_samples, row_samples, pivot_rows, rank_blocks, upper_inverse, upanel_left):
    width_local = col_samples.shape[2]
    ranks_max = row_samples.shape[2]
    offset = lax.axis_index("col") * width_local
    positions = offset + lax.broadcasted_iota(jnp.int32, (1, 1, width_local), 2)
    hits = (pivot_rows[:, :, None] == positions).astype(jnp.float32)
    flipped = jnp.swapaxes(col_samples, 2, 3)
    partial_entries = jnp.sum(flipped * hits[:, None], axis=3)
    entries = lax.psum(partial_entries, "col")
    levels = lax.broadcasted_iota(jnp.int32, (1, ranks_max), 1)
    keeping = (levels < RANK_STEP * rank_blocks[:, None]).astype(jnp.float32)
    magnitude = jnp.maximum(entries[:, 0] * entries[:, 0] + entries[:, 1] * entries[:, 1], 1.0)
    factor_real = keeping * entries[:, 0] / magnitude
    factor_imag = -keeping * entries[:, 1] / magnitude
    scaled = scale_rows(row_samples, factor_real, factor_imag)
    portion = lax.all_gather(upper_inverse, "row", axis=2, tiled=True)
    real_part, imag_part = complex_product(
        "trk,kn->trn", scaled[:, 0], scaled[:, 1], portion[0], portion[1]
    )
    partial_panel = jnp.stack((real_part, imag_part), axis=1)
    panel_full = lax.psum(partial_panel, "col")
    core_real, core_imag = complex_product(
        "trn,jns->tjrs", panel_full[:, 0], panel_full[:, 1], upanel_left[:, 0], upanel_left[:, 1]
    )
    cores = jnp.stack((core_real, core_imag), axis=2)
    panel_local = lax.dynamic_slice_in_dim(panel_full, offset, width_local, 3)
    return (panel_local, cores)


def solution(mesh):
    in_specs = (
        P("row", None, "col", None),
        P("row", None, None, "col"),
        P("row", None),
        P("row"),
        P(None, "col", "row"),
        P("col", None, None, None),
    )
    out_specs = (P("row", None, None, "col"), P("row", "col", None, None, None))
    return jax.shard_map(
        on_device, mesh=mesh, in_specs=in_specs, out_specs=out_specs, check_vma=False
    )
```

profile of v0, /device:TPU:0, one launch (start us, length us, event | category | flops | bytes accessed | tf_op | source)
XLA Modules:
  0.0 263.2 jit_solution(7308855048611063219)
XLA Ops:
  7.2 0.0 all-gather.2.cloned.1.call-start
  7.2 0.7 all-gather.2.cloned.1.call-update
  7.9 0.0 all-reduce.2.cloned.1.call-start
  8.0 0.8 compare_convert_fusion
  8.8 0.0 copy-start.3
  8.8 1.4 fusion.20
  10.2 13.5 %psum.14 = f32[2,2,128]{2,1,0:T(2,128)S(1)} all-reduce(f32[2,2,128]{2,1,0:T(2,128)S(1)} %fusion.20), channel_id=1, replica_groups=mesh['row'=8,'col'=4] {'col'}, use_global_device_ids=true, to_apply=%region_1.0 | all-reduce | flops 512 | bytes 4096 | tf_op jit(solution)/shard_map/psum | solution.py:41
  23.7 0.7 broadcast_multiply_fusion
  24.3 0.1 select_divide_fusion
  24.4 44.1 %all-gather.2.cloned.1.call-done = f32[2,512,2048]{2,1,0:T(8,128)} async-done(((f32[2,512,256]{2,1,0:T(8,128)}), f32[2,512,2048]{2,1,0:T(8,128)}) %all-gather.2.cloned.1.call-update) | async-done | bytes 8388624 | tf_op jit(solution)/shard_map/all_gather | solution.py:48
  68.5 0.0 copy-start
  68.5 5.9 %fusion = f32[2,128,2048]{2,1,0:T(8,128)S(1)} fusion(f32[2,512,2048]{2,1,0:T(8,128)} %all-gather.2.cloned.1.call-done, f32[2,2,128,512]{3,2,1,0:T(8,128)} %param.7, f32[2,128]{1,0:T(2,128)S(1)} %get-tuple-element.7, f32[2,128]{1,0:T(2,128)S(1)} %get-tuple-element.6), kind=kOutput, calls=%fused_computation.3 | convolution fusion | flops 3221618688 | bytes 7342080 | tf_op jit(solution)/shard_map/trk,kn->trn/dot_general | solution.py:12
  74.4 0.0 copy-done.3
  74.4 5.7 %fusion.1 = f32[2,128,2048]{2,1,0:T(8,128)S(1)} fusion(f32[2,512,2048]{2,1,0:T(8,128)} %all-gather.2.cloned.1.call-done, f32[2,2,128,512]{3,2,1,0:T(8,128)S(1)} %copy-done.3, f32[2,128]{1,0:T(2,128)S(1)} %get-tuple-element.7, f32[2,128]{1,0:T(2,128)S(1)} %get-tuple-element.6), kind=kOutput, calls=%fused_computation.4 | convolution fusion | flops 3221618688 | bytes 7342080 | tf_op jit(solution)/shard_map/trk,kn->trn/dot_general | solution.py:12
  80.1 0.0 copy-done
  80.1 3.8 %fusion.7 = f32[2,1,128,2048]{3,2,0,1:T(8,128)S(1)} fusion(f32[2,128,2048]{2,1,0:T(8,128)S(1)} %fusion, f32[2,512,2048]{2,1,0:T(8,128)S(1)} %copy-done, f32[2,2,128,512]{3,2,1,0:T(8,128)S(1)} %copy-done.3, f32[2,128]{1,0:T(2,128)S(1)} %get-tuple-element.7, f32[2,128]{1,0:T(2,128)S(1)} %get-tuple-element.6), kind=kOutput, calls=%fused_computation.10 | convolution fusion | flops 3222142976 | bytes 9439232 | tf_op jit(solution)/shard_map/trk,kn->trn/dot_general | solution.py:12
  84.0 3.8 %fusion.5 = f32[2,1,128,2048]{3,2,0,1:T(8,128)S(1)} fusion(f32[2,128,2048]{2,1,0:T(8,128)S(1)} %fusion.1, f32[2,512,2048]{2,1,0:T(8,128)S(1)} %copy-done, f32[2,2,128,512]{3,2,1,0:T(8,128)S(1)} %copy-done.3, f32[2,128]{1,0:T(2,128)S(1)} %get-tuple-element.7, f32[2,128]{1,0:T(2,128)S(1)} %get-tuple-element.6), kind=kOutput, calls=%fused_computation.8 | convolution fusion | flops 3222142976 | bytes 9439232 | tf_op jit(solution)/shard_map/trk,kn->trn/dot_general | solution.py:12
  87.8 2.5 pad_maximum_fusion
  90.2 0.0 copy-start.2
  90.2 0.0 all-reduce.2.cloned.1.call-update
  90.3 155.1 %all-reduce.2.cloned.1.call-done = f32[2,2,128,2048]{3,2,0,1:T(8,128)} async-done(((f32[2,2,128,2048]{3,2,0,1:T(8,128)}), f32[2,2,128,2048]{3,2,0,1:T(8,128)}) %all-reduce.2.cloned.1.call-update) | async-done | bytes 4194320 | tf_op jit(solution)/shard_map/psum | solution.py:53
  245.4 0.0 copy-start.1
  245.4 1.4 constant_dynamic-slice_fusion
  246.8 1.0 copy.11
  247.9 0.0 copy-done.2
  247.9 0.1 copy-done.1
  248.0 1.8 fusion.8
  249.8 1.8 fusion.9
  251.7 2.1 fusion.15
  253.8 1.8 fusion.13
  255.6 0.7 copy.12
  (3 shorter events, 0.0 us)
Async XLA Ops:
  7.2 61.3 %all-gather.2.cloned.1.call-start = ((), (), s32[]{:S(2)}) async-start(), calls=%async_computation | async-start | bytes 9437184 | tf_op jit(solution)/shard_map/all_gather | solution.py:48
  7.9 237.5 %all-reduce.2.cloned.1.call-start = ((), (), s32[]{:S(2)}) async-start(), calls=%async_computation.1 | async-start | bytes 8388608 | tf_op jit(solution)/shard_map/psum | solution.py:53
  8.8 65.6 %copy-start.3 = (f32[2,2,128,512]{3,2,1,0:T(8,128)S(1)}, f32[2,2,128,512]{3,2,1,0:T(8,128)}, u32[]{:S(2)}) copy-start(f32[2,2,128,512]{3,2,1,0:T(8,128)} %param.7) | copy-start | bytes 3145732
  68.5 11.7 %copy-start = (f32[2,512,2048]{2,1,0:T(8,128)S(1)}, f32[2,512,2048]{2,1,0:T(8,128)}, u32[]{:S(2)}) copy-start(f32[2,512,2048]{2,1,0:T(8,128)} %all-gather.2.cloned.1.call-done) | copy-start | bytes 25165828
  90.2 157.6 %copy-start.2 = (f32[1,2,2048,128]{3,2,1,0:T(8,128)S(1)}, f32[1,2,2048,128]{3,2,1,0:T(8,128)}, u32[]{:S(2)}) copy-start(f32[1,2,2048,128]{3,2,1,0:T(8,128)} %param.11) | copy-start | bytes 6291460
  245.4 2.6 copy-start.1
Sparse Core Ops, SparseCore 0:
  9.8 58.5 all-gather.1
  90.4 154.9 all-reduce.1
where the time goes:
time: 263 us
  waiting for transfers between devices  200 us (76%)
  matrix products  26.8 us (10%)
  between operations  14.2 us (5%)
  blocking collectives  13.5 us (5%)
  other arithmetic  5.43 us (2%)
  local copies, waits for them, and re-layouts  3.36 us (1%)
    psum x1, waiting for transfers between devices, on_device(): panel_full = lax.psum(partial_panel, 'col')  155 us
    all_gather x1, waiting for transfers between devices, on_device(): portion = lax.all_gather(upper_inverse, 'row', axis=2, tiled=True)  44.1 us
    dot_general x8, matrix products, single(): jnp.einsum(pattern, left, right, precision=lax.Precision.HIGHEST, preferr...  26.8 us
    psum x1, blocking collectives, on_device(): entries = lax.psum(partial_entries, 'col')  13.5 us
  transfers between devices with their start and end apart: 2, of which 2 were waited for; matrix products, arithmetic and copies ran while one was open for 1% of the time, Pallas kernels for 0%

commit v1 on v0

--- a/solution.py
+++ b/solution.py
@@ -50,7 +50,10 @@
         "trk,kn->trn", scaled[:, 0], scaled[:, 1], portion[0], portion[1]
     )
     partial_panel = jnp.stack((real_part, imag_part), axis=1)
-    panel_full = lax.psum(partial_panel, "col")
+    devs = lax.axis_size("col")
+    panel_full = partial_panel
+    for d in [[(to_i, to_i ^ k0) for to_i in range(devs)] for k0 in (1, 2, 4, 8, 16) if k0 < devs]:
+        panel_full = panel_full + lax.ppermute(panel_full, "col", d)
     core_real, core_imag = complex_product(
         "trn,jns->tjrs", panel_full[:, 0], panel_full[:, 1], upanel_left[:, 0], upanel_left[:, 1]
     )

time: 263 us -> 389 us (1.48)
  waiting for transfers between devices: 200 us -> 317 us
  other arithmetic: 5.43 us -> 11.9 us
  starting transfers between devices: 0.08 us -> 4 us
    ppermute x0 -> x2, waiting for transfers between devices: none -> 272 us  [on_device(): panel_full = panel_full + lax.ppermute(panel_full, 'col', d)]
    psum x1 -> x0, waiting for transfers between devices: 155 us -> none  [on_device(): panel_full = lax.psum(partial_panel, 'col')]
    add x0 -> x2, other arithmetic: none -> 8.52 us  [on_device(): panel_full = panel_full + lax.ppermute(panel_full, 'col', d)]
    ppermute x0 -> x2, starting transfers between devices: none -> 3.96 us  [on_device(): panel_full = panel_full + lax.ppermute(panel_full, 'col', d)]
  transfers between devices with their start and end apart: 2 -> 3, of which waited for: 2 -> 3; matrix products, arithmetic and copies ran while one was open for 1% -> 1% of each run, Pallas kernels for 0% -> 0%
where the time goes in v1:
time: 389 us
  waiting for transfers between devices  317 us (81%)
  matrix products  26.8 us (7%)
  between operations  14.2 us (4%)
  blocking collectives  13.5 us (3%)
  other arithmetic  11.9 us (3%)
  starting transfers between devices  4 us (1%)
    ppermute x2, waiting for transfers between devices, on_device(): panel_full = panel_full + lax.ppermute(panel_full, 'col', d)  272 us
    all_gather x1, waiting for transfers between devices, on_device(): portion = lax.all_gather(upper_inverse, 'row', axis=2, tiled=True)  44.1 us
    dot_general x8, matrix products, single(): jnp.einsum(pattern, left, right, precision=lax.Precision.HIGHEST, preferr...  26.8 us
    psum x1, blocking collectives, on_device(): entries = lax.psum(partial_entries, 'col')  13.5 us
    add x2, other arithmetic, on_device(): panel_full = panel_full + lax.ppermute(panel_full, 'col', d)  8.52 us
  transfers between devices with their start and end apart: 3, of which 3 were waited for; matrix products, arithmetic and copies ran while one was open for 1% of the time, Pallas kernels for 0%

profile of v1, /device:TPU:0, one launch (start us, length us, event | category | flops | bytes accessed | tf_op | source)
XLA Modules:
  0.0 388.8 jit_solution(2393113915347066796)
XLA Ops:
  7.2 0.0 all-gather.2.cloned.1.call-start
  7.2 0.7 all-gather.2.cloned.1.call-update
  7.9 0.8 compare_convert_fusion
  8.7 0.0 copy-start.4
  8.7 1.4 fusion.20
  10.1 13.5 %psum.7 = f32[2,2,128]{2,1,0:T(2,128)S(1)} all-reduce(f32[2,2,128]{2,1,0:T(2,128)S(1)} %fusion.20), channel_id=1, replica_groups=mesh['row'=8,'col'=4] {'col'}, use_global_device_ids=true, to_apply=%region_1.0 | all-reduce | flops 512 | bytes 4096 | tf_op jit(solution)/shard_map/psum | solution.py:41
  23.6 0.7 broadcast_multiply_fusion
  24.3 0.1 select_divide_fusion
  24.4 44.1 %all-gather.2.cloned.1.call-done = f32[2,512,2048]{2,1,0:T(8,128)} async-done(((f32[2,512,256]{2,1,0:T(8,128)}), f32[2,512,2048]{2,1,0:T(8,128)}) %all-gather.2.cloned.1.call-update) | async-done | bytes 8388624 | tf_op jit(solution)/shard_map/all_gather | solution.py:48
  68.5 5.9 %fusion = f32[2,128,2048]{2,1,0:T(8,128)S(1)} fusion(f32[2,512,2048]{2,1,0:T(8,128)} %all-gather.2.cloned.1.call-done, f32[2,2,128,512]{3,2,1,0:T(8,128)} %param.7, f32[2,128]{1,0:T(2,128)S(1)} %get-tuple-element.7, f32[2,128]{1,0:T(2,128)S(1)} %get-tuple-element.6), kind=kOutput, calls=%fused_computation.3 | convolution fusion | flops 3221618688 | bytes 7342080 | tf_op jit(solution)/shard_map/trk,kn->trn/dot_general | solution.py:12
  74.4 0.0 copy-done.4
  74.4 5.7 %fusion.1 = f32[2,128,2048]{2,1,0:T(8,128)S(1)} fusion(f32[2,512,2048]{2,1,0:T(8,128)} %all-gather.2.cloned.1.call-done, f32[2,2,128,512]{3,2,1,0:T(8,128)S(1)} %copy-done.4, f32[2,128]{1,0:T(2,128)S(1)} %get-tuple-element.7, f32[2,128]{1,0:T(2,128)S(1)} %get-tuple-element.6), kind=kOutput, calls=%fused_computation.4 | convolution fusion | flops 3221618688 | bytes 7342080 | tf_op jit(solution)/shard_map/trk,kn->trn/dot_general | solution.py:12
  80.1 0.0 copy-done
  80.1 3.8 fusion.7
  83.9 3.8 fusion.5
  87.7 0.0 copy-start.1
  87.8 0.4 pad_maximum_fusion
  88.1 1.6 collective-permute-start
  89.7 91.2 %collective-permute-done = f32[2,2,128,2048]{3,2,0,1:T(8,128)S(1)} collective-permute-done((f32[2,2,128,2048]{3,2,0,1:T(8,128)S(1)}, f32[2,2,128,2048]{3,2,0,1:T(8,128)S(1)}, u32[]{:S(2)}, u32[]{:S(2)}) %collective-permute-start) | collective-permute-done | bytes 4194336 | tf_op jit(solution)/shard_map/ppermute | solution.py:56
  180.9 3.1 fusion.29
  184.1 0.0 copy-done.1
  184.1 0.1 copy-done.2
  184.2 2.4 collective-permute-start.1
  186.6 180.6 %collective-permute-done.1 = f32[2,2,128,2048]{3,2,0,1:T(8,128)} collective-permute-done((f32[2,2,128,2048]{3,2,0,1:T(8,128)}, f32[2,2,128,2048]{3,2,0,1:T(8,128)}, u32[]{:S(2)}, u32[]{:S(2)}) %collective-permute-start.1) | collective-permute-done | bytes 4194336 | tf_op jit(solution)/shard_map/ppermute | solution.py:56
  367.1 5.4 %fusion.31 = f32[2,2,128,2048]{3,2,0,1:T(8,128)S(1)} fusion(f32[2,2,128,2048]{3,2,0,1:T(8,128)} %collective-permute-done.1, f32[2,2,128,2048]{3,2,0,1:T(8,128)} %copy-done.2, f32[2,1,128,2048]{3,2,0,1:T(8,128)S(1)} %fusion.7, f32[2,1,128,2048]{3,2,0,1:T(8,128)} %copy-done.1), kind=kLoop, calls=%fused_computation.48 | loop fusion | flops 3145728 | bytes 16777216 | tf_op jit(solution)/shard_map/add | solution.py:56
  372.5 1.8 fusion.10
  374.4 2.1 fusion.11
  376.4 1.8 fusion.15
  378.3 1.8 fusion.13
  380.1 0.1 constant_dynamic-slice_fusion
  380.2 1.0 copy.11
  381.3 0.7 copy.12
  (7 shorter events, 0.0 us)
Async XLA Ops:
  7.2 61.3 %all-gather.2.cloned.1.call-start = ((), (), s32[]{:S(2)}) async-start(), calls=%async_computation | async-start | bytes 9437184 | tf_op jit(solution)/shard_map/all_gather | solution.py:48
  8.7 65.7 %copy-start.4 = (f32[2,2,128,512]{3,2,1,0:T(8,128)S(1)}, f32[2,2,128,512]{3,2,1,0:T(8,128)}, u32[]{:S(2)}) copy-start(f32[2,2,128,512]{3,2,1,0:T(8,128)} %param.7) | copy-start | bytes 3145732
  68.5 11.7 %copy-start = (f32[2,512,2048]{2,1,0:T(8,128)S(1)}, f32[2,512,2048]{2,1,0:T(8,128)}, u32[]{:S(2)}) copy-start(f32[2,512,2048]{2,1,0:T(8,128)} %all-gather.2.cloned.1.call-done) | copy-start | bytes 25165828
  87.7 96.3 %copy-start.1 = (f32[2,1,128,2048]{3,2,0,1:T(8,128)}, f32[2,1,128,2048]{3,2,0,1:T(8,128)S(1)}, u32[]{:S(2)}) copy-start(f32[2,1,128,2048]{3,2,0,1:T(8,128)S(1)} %fusion.5) | copy-start | bytes 6291460
  88.1 92.8 %collective-permute-start = (f32[2,2,128,2048]{3,2,0,1:T(8,128)S(1)}, f32[2,2,128,2048]{3,2,0,1:T(8,128)S(1)}, u32[]{:S(2)}, u32[]{:S(2)}) collective-permute-start(f32[2,2,128,2048]{3,2,0,1:T(8,128)S(1)} %pad_maximum_fusion), channel_id=1, source_target_pairs={{0,1},{1,0},{2,3},{3,2},{4,5},{5,4},{6,7},{7,6},{8,9},{9,8},{10,11... | collective-permute-start | bytes 12582920 | tf_op jit(solution)/shard_map/ppermute | solution.py:56
  180.9 3.2 copy-start.2
  184.2 183.0 %collective-permute-start.1 = (f32[2,2,128,2048]{3,2,0,1:T(8,128)}, f32[2,2,128,2048]{3,2,0,1:T(8,128)}, u32[]{:S(2)}, u32[]{:S(2)}) collective-permute-start(f32[2,2,128,2048]{3,2,0,1:T(8,128)} %fusion.29), channel_id=1, source_target_pairs={{0,2},{1,3},{2,0},{3,1},{4,6},{5,7},{6,4},{7,5},{8,10},{9,11},{10,... | collective-permute-start | bytes 12582920 | tf_op jit(solution)/shard_map/ppermute | solution.py:56
  186.6 186.0 %copy-start.3 = (f32[1,2,2048,128]{3,2,1,0:T(8,128)S(1)}, f32[1,2,2048,128]{3,2,1,0:T(8,128)}, u32[]{:S(2)}) copy-start(f32[1,2,2048,128]{3,2,1,0:T(8,128)} %param.11) | copy-start | bytes 6291460
Sparse Core Ops, SparseCore 0:
  9.8 58.5 all-gather.1

commit v2 on v0

--- a/solution.py
+++ b/solution.py
@@ -4,6 +4,11 @@
 from jax.sharding import PartitionSpec as P
 
 RANK_STEP = 16
+
+
+def all_parts(shard, name, along):
+    blocks = lax.all_gather(shard, name)
+    return jnp.concatenate(blocks, axis=along)
 
 
 def complex_product(pattern, left_real, left_imag, right_real, right_imag):
@@ -45,7 +50,7 @@
     factor_real = keeping * entries[:, 0] / magnitude
     factor_imag = -keeping * entries[:, 1] / magnitude
     scaled = scale_rows(row_samples, factor_real, factor_imag)
-    portion = lax.all_gather(upper_inverse, "row", axis=2, tiled=True)
+    portion = all_parts(upper_inverse, "row", 2)
     real_part, imag_part = complex_product(
         "trk,kn->trn", scaled[:, 0], scaled[:, 1], portion[0], portion[1]
     )

time: 263 us -> 282 us (1.072)
  local copies, waits for them, and re-layouts: 3.36 us -> 25.3 us
    squeeze x0 -> x2, local copies, waits for them, and re-layouts: none -> 9.85 us  [the longest x1 4.98 us: on_device(): portion[0]]
    all_gather x0 -> x1, local copies, waits for them, and re-layouts: none -> 8.24 us  [all_parts(): blocks = lax.all_gather(shard, name)]
    slice x0 -> x1, local copies, waits for them, and re-layouts: none -> 3.81 us  [on_device(): portion[0]]
where the time goes in v2:
time: 282 us
  waiting for transfers between devices  198 us (70%)
  local copies, waits for them, and re-layouts  25.3 us (9%)
  matrix products  24.8 us (9%)
  between operations  14.2 us (5%)
  blocking collectives  13.5 us (5%)
  other arithmetic  5.35 us (2%)
    psum x1, waiting for transfers between devices, on_device(): panel_full = lax.psum(partial_panel, 'col')  155 us
    all_gather x1, waiting for transfers between devices, all_parts(): blocks = lax.all_gather(shard, name)  42.6 us
    dot_general x8, matrix products, single(): jnp.einsum(pattern, left, right, precision=lax.Precision.HIGHEST, preferr...  24.8 us
    psum x1, blocking collectives, on_device(): entries = lax.psum(partial_entries, 'col')  13.5 us
    all_gather x1, local copies, waits for them, and re-layouts, all_parts(): blocks = lax.all_gather(shard, name)  8.24 us
  transfers between devices with their start and end apart: 2, of which 2 were waited for; matrix products, arithmetic and copies ran while one was open for 1% of the time, Pallas kernels for 0%

profile of v2, /device:TPU:0, one launch (start us, length us, event | category | flops | bytes accessed | tf_op | source)
XLA Modules:
  0.0 281.5 jit_solution(16148595749896217609)
XLA Ops:
  7.2 0.0 all-gather.3.cloned.1.call-start
  7.2 0.7 all-gather.3.cloned.1.call-update
  7.9 0.0 all-reduce.2.cloned.1.call-start
  8.0 0.8 compare_convert_fusion
  8.8 1.3 fusion.14
  10.1 13.5 %psum.14 = f32[2,2,128]{2,1,0:T(2,128)S(1)} all-reduce(f32[2,2,128]{2,1,0:T(2,128)S(1)} %fusion.14), channel_id=1, replica_groups=mesh['row'=8,'col'=4] {'col'}, use_global_device_ids=true, to_apply=%region_1.0 | all-reduce | flops 512 | bytes 4096 | tf_op jit(solution)/shard_map/psum | solution.py:46
  23.6 0.7 broadcast_multiply_fusion
  24.2 0.1 select_divide_fusion
  24.3 42.6 %all-gather.3.cloned.1.call-done = f32[16,512,256]{2,1,0:T(8,128)} async-done(((f32[2,512,256]{2,1,0:T(8,128)}), f32[16,512,256]{2,1,0:T(8,128)}) %all-gather.3.cloned.1.call-update) | async-done | bytes 8388624 | tf_op jit(solution)/shard_map/all_gather | solution.py:10
  66.9 8.2 %copy.17 = f32[8,2,512,256]{3,0,2,1:T(8,128)S(1)} copy(f32[8,2,512,256]{3,2,1,0:T(8,128)} %bitcast.81) | data formatting | bytes 16777216 | tf_op jit(solution)/shard_map/all_gather | solution.py:10
  75.1 3.8 %fusion.25 = (f32[1,512,8,256]{3,2,1,0:T(8,128)}, f32[1,512,8,256]{3,2,1,0:T(8,128)}) fusion(f32[2,512,8,256]{3,2,1,0:T(8,128)S(1)} %bitcast.80), kind=kLoop, calls=%fused_computation.43 | loop fusion | bytes 16777216 | tf_op jit(solution)/shard_map/slice | solution.py:55
  78.9 4.9 %reshape.116 = f32[512,2048,1]{1,0,2:T(8,128)} reshape(f32[1,512,8,256]{3,2,1,0:T(8,128)} %get-tuple-element.7) | data formatting | bytes 8388608 | tf_op jit(solution)/shard_map/squeeze | solution.py:55
  83.8 5.0 %reshape.115 = f32[512,2048,1]{1,0,2:T(8,128)} reshape(f32[1,512,8,256]{3,2,1,0:T(8,128)} %get-tuple-element.6) | data formatting | bytes 8388608 | tf_op jit(solution)/shard_map/squeeze | solution.py:55
  88.8 0.0 copy-done.4
  88.8 5.8 %fusion.21 = f32[2,128,2048]{2,1,0:T(8,128)S(1)} fusion(f32[512,2048,1]{1,0,2:T(8,128)} %reshape.116, f32[2,2,128,512]{3,2,1,0:T(8,128)S(1)} %copy-done.4, f32[2,128]{1,0:T(2,128)S(1)} %get-tuple-element.9, f32[2,128]{1,0:T(2,128)S(1)} %get-tuple-element.8), kind=kOutput, calls=%fused_computation.28 | convolution fusion | flops 3221618688 | bytes 7342080 | tf_op jit(solution)/shard_map/trk,kn->trn/dot_general | solution.py:17
  94.6 0.0 copy-done.1
  94.6 3.8 %fusion.23 = f32[2,128,2048]{2,1,0:T(8,128)S(1)} fusion(f32[512,2048,1]{1,0,2:T(8,128)S(1)} %copy-done.1, f32[2,2,128,512]{3,2,1,0:T(8,128)S(1)} %copy-done.4, f32[2,128]{1,0:T(2,128)S(1)} %get-tuple-element.9, f32[2,128]{1,0:T(2,128)S(1)} %get-tuple-element.8), kind=kOutput, calls=%fused_computation.30 | convolution fusion | flops 3221618688 | bytes 7342080 | tf_op jit(solution)/shard_map/trk,kn->trn/dot_general | solution.py:17
  98.4 0.0 copy-start
  98.4 3.8 %fusion = f32[2,1,128,2048]{3,2,0,1:T(8,128)S(1)} fusion(f32[2,128,2048]{2,1,0:T(8,128)S(1)} %fusion.21, f32[512,2048,1]{1,0,2:T(8,128)S(1)} %copy-done.1, f32[2,2,128,512]{3,2,1,0:T(8,128)S(1)} %copy-done.4, f32[2,128]{1,0:T(2,128)S(1)} %get-tuple-element.9, f32[2,128]{1,0:T(2,128)S(1)} %get-tuple-element.8), kind=kOutput, calls=%fused_computation.3 | convolution fusion | flops 3222142976 | bytes 9439232 | tf_op jit(solution)/shard_map/trk,kn->trn/dot_general | solution.py:17
  102.2 0.0 copy-done
  102.3 3.8 %fusion.1 = f32[2,1,128,2048]{3,2,0,1:T(8,128)S(1)} fusion(f32[2,128,2048]{2,1,0:T(8,128)S(1)} %fusion.23, f32[512,2048,1]{1,0,2:T(8,128)S(1)} %copy-done, f32[2,2,128,512]{3,2,1,0:T(8,128)S(1)} %copy-done.4, f32[2,128]{1,0:T(2,128)S(1)} %get-tuple-element.9, f32[2,128]{1,0:T(2,128)S(1)} %get-tuple-element.8), kind=kOutput, calls=%fused_computation.5 | convolution fusion | flops 3222142976 | bytes 9439232 | tf_op jit(solution)/shard_map/trk,kn->trn/dot_general | solution.py:17
  106.1 2.5 pad_maximum_fusion
  108.6 0.0 all-reduce.2.cloned.1.call-update
  108.6 155.1 %all-reduce.2.cloned.1.call-done = f32[2,2,128,2048]{3,2,0,1:T(8,128)} async-done(((f32[2,2,128,2048]{3,2,0,1:T(8,128)}), f32[2,2,128,2048]{3,2,0,1:T(8,128)}) %all-reduce.2.cloned.1.call-update) | async-done | bytes 4194320 | tf_op jit(solution)/shard_map/psum | solution.py:58
  263.7 1.4 constant_dynamic-slice_fusion
  265.2 1.0 copy.13
  266.2 0.1 copy-done.2
  266.3 2.1 fusion.2
  268.4 1.8 fusion.3
  270.2 1.9 fusion.9
  272.1 1.8 fusion.7
  274.0 0.7 copy.14
  (8 shorter events, 0.0 us)
Async XLA Ops:
  7.2 59.7 %all-gather.3.cloned.1.call-start = ((), (), s32[]{:S(2)}) async-start(), calls=%async_computation.1 | async-start | bytes 9437184 | tf_op jit(solution)/shard_map/all_gather | solution.py:10
  7.9 255.8 %all-reduce.2.cloned.1.call-start = ((), (), s32[]{:S(2)}) async-start(), calls=%async_computation | async-start | bytes 8388608 | tf_op jit(solution)/shard_map/psum | solution.py:58
  83.8 5.0 %copy-start.4 = (f32[2,2,128,512]{3,2,1,0:T(8,128)S(1)}, f32[2,2,128,512]{3,2,1,0:T(8,128)}, u32[]{:S(2)}) copy-start(f32[2,2,128,512]{3,2,1,0:T(8,128)} %param.7) | copy-start | bytes 3145732
  88.8 5.9 %copy-start.1 = (f32[512,2048,1]{1,0,2:T(8,128)S(1)}, f32[512,2048,1]{1,0,2:T(8,128)}, u32[]{:S(2)}) copy-start(f32[512,2048,1]{1,0,2:T(8,128)} %reshape.115) | copy-start | bytes 12582916
  98.4 3.8 %copy-start = (f32[512,2048,1]{1,0,2:T(8,128)S(1)}, f32[512,2048,1]{1,0,2:T(8,128)}, u32[]{:S(2)}) copy-start(f32[512,2048,1]{1,0,2:T(8,128)} %reshape.116) | copy-start | bytes 12582916
  108.5 157.6 %copy-start.3 = (f32[1,2,2048,128]{3,2,1,0:T(8,128)S(1)}, f32[1,2,2048,128]{3,2,1,0:T(8,128)}, u32[]{:S(2)}) copy-start(f32[1,2,2048,128]{3,2,1,0:T(8,128)} %param.11) | copy-start | bytes 6291460
  263.7 2.6 copy-start.2
Sparse Core Ops, SparseCore 0:
  9.9 56.9 all-gather.2
  108.7 154.9 all-reduce.1
